TPU v7x, 512 devices: a whole 4x4x16 slice. The times are simulated.
512 devices in a mesh: head: 8 (over y, core), frame: 64 (over x, z).
Axes of the slice: x: 4, y: 4, z: 16, core: 2. Of those that a mesh axis runs over, the one named last changes fastest.
Arguments:
- queries: bfloat16 [65536, 16, 128], P(('frame', 'head')), may hold values from -30 to 30
- keys: bfloat16 [65536, 16, 128], P(('frame', 'head')), may hold values from -4 to 4
- values: bfloat16 [65536, 16, 128], P(('frame', 'head')), may hold values from -24 to 24
- block_mask: int32 [64, 16, 16], replicated, may hold values from 0 to 1, as said below
- strides: int32 [64], replicated, may hold values from 1 to 16, as said below
- offsets: int32 [64], replicated, may hold values from 0 to 15
Outputs:
- attended: bfloat16 [65536, 16, 128], P(('frame', 'head'))
Inputs may be any that keep to these rules, and one draw needn't show every extreme that they name: Every diagonal entry block_mask[i, b, b] is 1. strides[0] is 1, strides[1] is 4, 8 or 16, and every later entry is 8 or 16.
All inputs are finite; a program needn't handle non-finite values.
Results may differ from a plain program's by a relative error of at most 0.0043.
Values may be sent and summed in bfloat16 or wider, within the bound.
No kernel may reach another device: no remote copies, remote signals or barrier semaphores. Data moves between devices by JAX's collectives and lax.ppermute only.
A program may use at most 64 MiB of HBM per device.

v0:
```python
import jax
import jax.numpy as jnp
from jax import lax
from jax.sharding import PartitionSpec as P

masked_score = -1e30


def passed_along(block, axis, distance):
    devices = range(lax.axis_size(axis))
    route = [(i - distance, i) for i in devices if i - distance in devices]
    return lax.ppermute(block, axis, route)


def group_terms(query_blocks, key_rows, value_rows, keep_mask, score_scale):
    scores = (
        jnp.einsum("qahd,gnhd->hqagn", query_blocks, key_rows, preferred_element_type=jnp.float32)
        * score_scale
    )
    allowed = keep_mask[None, :, None, :, :]
    scores = jnp.where(allowed, scores, masked_score)
    group_tops = jnp.max(scores, axis=4)
    weights = jnp.where(allowed, jnp.exp(scores - group_tops[..., None]), 0.0)
    group_totals = jnp.sum(weights, axis=4)
    group_sums = jnp.einsum(
        "hqagn,gnhd->hqagd",
        weights.astype(jnp.bfloat16),
        value_rows,
        preferred_element_type=jnp.float32,
    )
    return (group_tops, group_totals, group_sums)


def absorb(carry_state, group_tops, group_totals, group_sums):
    running_top, running_total, running_sum = carry_state
    new_top = jnp.maximum(running_top, jnp.max(group_tops, axis=3))
    shrink = jnp.exp(running_top - new_top)
    factors = jnp.exp(group_tops - new_top[..., None])
    running_total = running_total * shrink + jnp.sum(factors * group_totals, axis=3)
    running_sum = running_sum * shrink[..., None] + jnp.sum(factors[..., None] * group_sums, axis=3)
    return (new_top, running_total, running_sum)


def pick_blocks(key_blocks, value_blocks, offsets, source_frame, spacing, block_count):
    first_block = (spacing - offsets[source_frame] % spacing) % spacing
    chosen = first_block + spacing * jnp.arange(block_count, dtype=jnp.int32)
    return jnp.stack([jnp.take(key_blocks, chosen, axis=0), jnp.take(value_blocks, chosen, axis=0)])


def local(queries, keys, values, block_mask, strides, offsets):
    local_queries, local_keys, local_values = (
        lax.all_to_all(queries, "head", split_axis=1, concat_axis=0, tiled=True),
        lax.all_to_all(keys, "head", split_axis=1, concat_axis=0, tiled=True),
        lax.all_to_all(values, "head", split_axis=1, concat_axis=0, tiled=True),
    )
    frame_rows, heads_here, head_dim = local_queries.shape
    frame_blocks = block_mask.shape[1]
    block_rows = frame_rows // frame_blocks
    score_scale = head_dim ** (-0.5)
    frame_index = lax.axis_index("frame")
    frame_total = lax.axis_size("frame")
    query_blocks = local_queries.reshape(frame_blocks, block_rows, heads_here, head_dim)
    key_blocks = local_keys.reshape(frame_blocks, block_rows, heads_here, head_dim)
    value_blocks = local_values.reshape(frame_blocks, block_rows, heads_here, head_dim)
    own_mask = lax.dynamic_index_in_dim(block_mask, frame_index, 0, keepdims=False) == 1
    carry_state = (
        jnp.full((heads_here, frame_blocks, block_rows), masked_score, jnp.float32),
        jnp.zeros((heads_here, frame_blocks, block_rows), jnp.float32),
        jnp.zeros((heads_here, frame_blocks, block_rows, head_dim), jnp.float32),
    )
    half_blocks = frame_blocks // 2
    whole_keys = local_keys.reshape(1, frame_rows, heads_here, head_dim)
    whole_values = local_values.reshape(1, frame_rows, heads_here, head_dim)
    results = []
    for first_block in (0, half_blocks):
        keep_mask = jnp.repeat(
            own_mask[first_block : first_block + half_blocks], block_rows, axis=1
        )[:, None, :]
        results.append(
            group_terms(
                query_blocks[first_block : first_block + half_blocks],
                whole_keys,
                whole_values,
                keep_mask,
                score_scale,
            )
        )
    carry_state = absorb(
        carry_state,
        jnp.concatenate([entry[0] for entry in results], axis=1),
        jnp.concatenate([entry[1] for entry in results], axis=1),
        jnp.concatenate([entry[2] for entry in results], axis=1),
    )
    for distance in (1, 2, 3):
        spacing = frame_blocks // 4 if distance == 1 else frame_blocks // 2
        block_count = frame_blocks // spacing
        packed = pick_blocks(key_blocks, value_blocks, offsets, frame_index, spacing, block_count)
        for direction in (1, -1):
            arrived = passed_along(packed, "frame", direction * distance)
            source_frame = frame_index - direction * distance
            valid = (source_frame >= 0) & (source_frame < frame_total)
            clipped = jnp.clip(source_frame, 0, frame_total - 1)
            chosen = (spacing - offsets[clipped] % spacing) % spacing + spacing * jnp.arange(
                block_count, dtype=jnp.int32
            )
            attend_phase_ok = (chosen + offsets[clipped]) % strides[distance] == 0
            attend_kept = valid & own_mask[:, chosen] & attend_phase_ok[None, :]
            attend_keep_mask = jnp.repeat(attend_kept, block_rows, axis=1)[:, None, :]
            near_keys = arrived[0].reshape(1, block_count * block_rows, heads_here, head_dim)
            near_values = arrived[1].reshape(1, block_count * block_rows, heads_here, head_dim)
            carry_state = absorb(
                carry_state,
                *group_terms(query_blocks, near_keys, near_values, attend_keep_mask, score_scale)
            )
    anchor_block = (frame_blocks - offsets[frame_index] % frame_blocks) % frame_blocks
    anchor_pair = jnp.stack([key_blocks[anchor_block], value_blocks[anchor_block]])[None]
    gathered = lax.all_gather(anchor_pair, "frame", axis=0, tiled=True)
    piece_frames = gathered.shape[0]
    group_width = 4
    grouped = gathered.reshape(
        piece_frames // group_width, group_width, 2, block_rows, heads_here, head_dim
    )

    def one_group(state_inner, entry):
        group_blocks, group_number = entry
        sources = 0 + group_number * group_width + jnp.arange(group_width, dtype=jnp.int32)
        distances = jnp.abs(frame_index - sources)
        spots = (frame_blocks - offsets[sources] % frame_blocks) % frame_blocks
        phase_ok = (spots + offsets[sources]) % strides[distances] == 0
        kept = (distances >= 4)[None, :] & own_mask[:, spots] & phase_ok[None, :]
        keep_mask = jnp.repeat(kept, block_rows, axis=1).reshape(
            frame_blocks, group_width, block_rows
        )
        terms = group_terms(
            query_blocks, group_blocks[:, 0], group_blocks[:, 1], keep_mask, score_scale
        )
        return (absorb(state_inner, *terms), None)

    numbers = jnp.arange(piece_frames // group_width, dtype=jnp.int32)
    state_out, unused = lax.scan(one_group, carry_state, (grouped, numbers))
    carry_state = state_out
    running_top, running_total, running_sum = carry_state
    output = (running_sum / running_total[..., None]).astype(jnp.bfloat16)
    output = jnp.transpose(output, (1, 2, 0, 3)).reshape(frame_rows, heads_here, head_dim)
    return lax.all_to_all(output, "head", split_axis=0, concat_axis=1, tiled=True)


def solution(mesh):
    placed = (
        P(("frame", "head"), None, None),
        P(("frame", "head"), None, None),
        P(("frame", "head"), None, None),
        P(),
        P(),
        P(),
    )
    return jax.shard_map(
        local,
        mesh=mesh,
        in_specs=placed,
        out_specs=P(("frame", "head"), None, None),
        check_vma=False,
    )
```

profile of v0, /device:TPU:1, one launch (start us, length us, event | category | flops | bytes accessed | tf_op | source)
XLA Modules:
  0.0 511.0 jit_solution(10326645621186077479)
XLA Ops:
  6.5 2.0 copy.119
  8.6 10.2 %all-to-all-start.1 = ((bf16[128,16,128]{2,0,1:T(8,128)(2,1)}), bf16[128,16,128]{2,0,1:T(8,128)(2,1)S(1)}, u32[]{:S(2)}, u32[]{:S(2)}) async-start(bf16[128,16,128]{2,0,1:T(8,128)(2,1)} %copy.119), calls=%async_computation.1 | async-start | bytes 1048576 | tf_op jit(solution)/shard_map/all_to_all | solution.py:53
  46.7 2.0 copy.125
  49.3 4.8 all-to-all-start.2
  61.0 2.5 all-to-all-done.2
  63.5 4.4 all-to-all-start
  71.7 4.0 collective-permute-start
  75.8 1.9 collective-permute-start.2
  79.0 7.0 %collective-permute-start.4 = (bf16[2,2,64,2,128]{4,2,3,1,0:T(8,128)(2,1)S(1)}, bf16[2,2,64,2,128]{4,2,3,1,0:T(8,128)(2,1)S(1)}, u32[]{:S(2)}, u32[]{:S(2)}) collective-permute-start(bf16[2,2,64,2,128]{4,2,3,1,0:T(8,128)(2,1)S(1)} %pad_maximum_fusion.1), channel_id=1, source_target_pairs={{0,3},{1,4},{2,5},{3,6},{4,7},{5,8},{6,9},{7,10},{8,11},{9,12},{10... | collective-permute-start | bytes 393224 | tf_op jit(solution)/shard_map/ppermute | solution.py:12
  90.2 2.7 fusion.21
  97.3 7.7 %collective-permute-done.3 = bf16[2,2,64,2,128]{4,2,3,1,0:T(8,128)(2,1)S(1)} collective-permute-done((bf16[2,2,64,2,128]{4,2,3,1,0:T(8,128)(2,1)S(1)}, bf16[2,2,64,2,128]{4,2,3,1,0:T(8,128)(2,1)S(1)}, u32[]{:S(2)}, u32[]{:S(2)}) %collective-permute-start.3) | collective-permute-done | bytes 131104 | tf_op jit(solution)/shard_map/ppermute | solution.py:12
  119.0 1.7 fusion.46
  120.8 3.0 fusion.58
  123.7 103.3 %all-gather.3.cloned.1.call-done = bf16[128,64,2,128]{3,1,0,2:T(8,128)(2,1)} async-done(((bf16[2,64,2,128]{3,1,0,2:T(8,128)(2,1)}), bf16[128,64,2,128]{3,1,0,2:T(8,128)(2,1)}) %all-gather.3.cloned.1.call-update) | async-done | bytes 4194320 | tf_op jit(solution)/shard_map/all_gather | solution.py:117
  227.0 250.4 %while.16 = (s32[]{:T(128)}, f32[2,16,64]{2,1,0:T(8,128)S(1)}, f32[2,16,64]{2,1,0:T(8,128)S(1)}, f32[2,16,64,128]{3,2,1,0:T(8,128)}, s32[]{:T(128)}, /*index=5*/...) while((s32[]{:T(128)}, f32[2,16,64]{2,1,0:T(8,128)S(1)}, ...), condition=%wide.region_22.25_spmd, body=%wide.region_16.24_spmd.sunk | while | flops 276053440 | bytes 31036728 | solution.py:140
  232.4 2.4 fusion.229
  234.9 2.7 copy.175
  237.5 2.3 fusion.230
  248.1 2.4 fusion.229
  250.5 2.7 copy.175
  253.2 2.3 fusion.230
  263.7 2.4 fusion.229
  266.2 2.7 copy.175
  268.8 2.3 fusion.230
  279.4 2.4 fusion.229
  281.8 2.7 copy.175
  284.5 2.3 fusion.230
  295.0 2.4 fusion.229
  297.5 2.7 copy.175
  300.1 2.3 fusion.230
  310.7 2.4 fusion.229
  313.1 2.7 copy.175
  315.8 2.3 fusion.230
  326.3 2.4 fusion.229
  328.8 2.7 copy.175
  331.4 2.3 fusion.230
  342.0 2.4 fusion.229
  344.4 2.7 copy.175
  347.1 2.3 fusion.230
  357.6 2.4 fusion.229
  360.1 2.7 copy.175
  362.7 2.3 fusion.230
  373.3 2.4 fusion.229
  375.7 2.7 copy.175
  378.4 2.3 fusion.230
  388.9 2.4 fusion.229
  391.4 2.7 copy.175
  394.0 2.3 fusion.230
  404.5 2.4 fusion.229
  407.0 2.7 copy.175
  409.7 2.3 fusion.230
  420.2 2.4 fusion.229
  422.7 2.7 copy.175
  425.3 2.3 fusion.230
  435.8 2.4 fusion.229
  438.3 2.7 copy.175
  441.0 2.3 fusion.230
  451.5 2.4 fusion.229
  453.9 2.7 copy.175
  456.6 2.3 fusion.230
  467.1 2.4 fusion.229
  469.6 2.7 copy.175
  472.3 2.3 fusion.230
  479.5 23.4 %all_to_all.63 = bf16[1024,2,128]{2,1,0:T(2,128)(2,1)S(1)} all-to-all(bf16[1024,2,128]{2,1,0:T(2,128)(2,1)S(1)} %bitcast.475), channel_id=1, replica_groups=mesh['head'=8,'frame'=64] {'head'}, dimensions={0} | all-to-all | bytes 1048576 | tf_op jit(solution)/shard_map/all_to_all | solution.py:145
  (548 shorter events, 170.1 us)
Async XLA Ops:
  6.5 33.9 %copy-start = (s32[64,16,16]{0,2,1:T(8,128)S(1)}, s32[64,16,16]{0,2,1:T(8,128)}, u32[]{:S(2)}) copy-start(s32[64,16,16]{0,2,1:T(8,128)} %param.15) | copy-start | bytes 196612
  6.5 47.7 %copy-start.5 = (bf16[128,16,128]{2,1,0:T(8,128)(2,1)S(1)}, bf16[128,16,128]{2,1,0:T(8,128)(2,1)}, u32[]{:S(2)}) copy-start(bf16[128,16,128]{2,1,0:T(8,128)(2,1)} %param.12) | copy-start | bytes 1572868
  8.6 40.7 %all-to-all-start.1 = ((bf16[128,16,128]{2,0,1:T(8,128)(2,1)}), bf16[128,16,128]{2,0,1:T(8,128)(2,1)S(1)}, u32[]{:S(2)}, u32[]{:S(2)}) async-start(bf16[128,16,128]{2,0,1:T(8,128)(2,1)} %copy.119), calls=%async_computation.1 | async-start | bytes 1048576 | tf_op jit(solution)/shard_map/all_to_all | solution.py:53
  49.3 14.2 %all-to-all-start.2 = ((bf16[128,16,128]{2,0,1:T(8,128)(2,1)}), bf16[128,16,128]{2,0,1:T(8,128)(2,1)S(1)}, u32[]{:S(2)}, u32[]{:S(2)}) async-start(bf16[128,16,128]{2,0,1:T(8,128)(2,1)} %copy.125), calls=%async_computation.2 | async-start | bytes 1048576 | tf_op jit(solution)/shard_map/all_to_all | solution.py:54
  63.5 22.5 %all-to-all-start = ((bf16[128,16,128]{2,0,1:T(8,128)(2,1)}), bf16[128,16,128]{2,0,1:T(8,128)(2,1)S(1)}, u32[]{:S(2)}, u32[]{:S(2)}) async-start(bf16[128,16,128]{2,0,1:T(8,128)(2,1)} %copy.117), calls=%async_computation | async-start | bytes 1048576 | tf_op jit(solution)/shard_map/all_to_all | solution.py:52
  67.8 159.2 %all-gather.3.cloned.1.call-start = ((), (), s32[]{:S(2)}) async-start(), calls=%async_computation.4 | async-start | bytes 4259840 | tf_op jit(solution)/shard_map/all_gather | solution.py:117
  70.4 40.1 %collective-permute-start.1 = (bf16[2,4,64,2,128]{4,2,3,1,0:T(8,128)(2,1)S(1)}, bf16[2,4,64,2,128]{4,2,3,1,0:T(8,128)(2,1)S(1)}, u32[]{:S(2)}, u32[]{:S(2)}) collective-permute-start(bf16[2,4,64,2,128]{4,2,3,1,0:T(8,128)(2,1)S(1)} %pad_maximum_fusion), channel_id=1, source_target_pairs={{1,0},{2,1},{3,2},{4,3},{5,4},{6,5},{7,6},{8,7},{9,8},{10,9},{11,1... | collective-permute-start | bytes 786440 | tf_op jit(solution)/shard_map/ppermute | solution.py:12
  71.7 38.8 %collective-permute-start = (bf16[2,4,64,2,128]{4,2,3,1,0:T(8,128)(2,1)S(1)}, bf16[2,4,64,2,128]{4,2,3,1,0:T(8,128)(2,1)S(1)}, u32[]{:S(2)}, u32[]{:S(2)}) collective-permute-start(bf16[2,4,64,2,128]{4,2,3,1,0:T(8,128)(2,1)S(1)} %pad_maximum_fusion), channel_id=1, source_target_pairs={{0,1},{1,2},{2,3},{3,4},{4,5},{5,6},{6,7},{7,8},{8,9},{9,10},{10,1... | collective-permute-start | bytes 786440 | tf_op jit(solution)/shard_map/ppermute | solution.py:12
  75.8 18.2 %collective-permute-start.2 = (bf16[2,2,64,2,128]{4,2,3,1,0:T(8,128)(2,1)S(1)}, bf16[2,2,64,2,128]{4,2,3,1,0:T(8,128)(2,1)}, u32[]{:S(2)}, u32[]{:S(2)}) collective-permute-start(bf16[2,2,64,2,128]{4,2,3,1,0:T(8,128)(2,1)S(1)} %pad_maximum_fusion.1), channel_id=1, source_target_pairs={{0,2},{1,3},{2,4},{3,5},{4,6},{5,7},{6,8},{7,9},{8,10},{9,11},{10,... | collective-permute-start | bytes 393224 | tf_op jit(solution)/shard_map/ppermute | solution.py:12
  77.7 18.7 %collective-permute-start.5 = (bf16[2,2,64,2,128]{4,2,3,1,0:T(8,128)(2,1)S(1)}, bf16[2,2,64,2,128]{4,2,3,1,0:T(8,128)(2,1)}, u32[]{:S(2)}, u32[]{:S(2)}) collective-permute-start(bf16[2,2,64,2,128]{4,2,3,1,0:T(8,128)(2,1)S(1)} %pad_maximum_fusion.1), channel_id=1, source_target_pairs={{3,0},{4,1},{5,2},{6,3},{7,4},{8,5},{9,6},{10,7},{11,8},{12,9},{13... | collective-permute-start | bytes 393224 | tf_op jit(solution)/shard_map/ppermute | solution.py:12
  79.0 18.3 %collective-permute-start.4 = (bf16[2,2,64,2,128]{4,2,3,1,0:T(8,128)(2,1)S(1)}, bf16[2,2,64,2,128]{4,2,3,1,0:T(8,128)(2,1)S(1)}, u32[]{:S(2)}, u32[]{:S(2)}) collective-permute-start(bf16[2,2,64,2,128]{4,2,3,1,0:T(8,128)(2,1)S(1)} %pad_maximum_fusion.1), channel_id=1, source_target_pairs={{0,3},{1,4},{2,5},{3,6},{4,7},{5,8},{6,9},{7,10},{8,11},{9,12},{10... | collective-permute-start | bytes 393224 | tf_op jit(solution)/shard_map/ppermute | solution.py:12
  89.2 1.1 copy-start.6
  92.9 12.5 %copy-start.11 = (pred[16,128]{1,0:T(8,128)(4,1)S(1)}, pred[16,128]{1,0:T(8,128)(4,1)}, u32[]{:S(2)}) copy-start(pred[16,128]{1,0:T(8,128)(4,1)} %broadcast_in_dim.280) | copy-start | bytes 6148
  94.0 12.1 %copy-start.9 = (pred[16,128]{1,0:T(8,128)(4,1)S(1)}, pred[16,128]{1,0:T(8,128)(4,1)}, u32[]{:S(2)}) copy-start(pred[16,128]{1,0:T(8,128)(4,1)} %broadcast_in_dim.277) | copy-start | bytes 6148
  94.0 11.1 %collective-permute-start.3 = (bf16[2,2,64,2,128]{4,2,3,1,0:T(8,128)(2,1)S(1)}, bf16[2,2,64,2,128]{4,2,3,1,0:T(8,128)(2,1)S(1)}, u32[]{:S(2)}, u32[]{:S(2)}) collective-permute-start(bf16[2,2,64,2,128]{4,2,3,1,0:T(8,128)(2,1)S(1)} %pad_maximum_fusion.1), channel_id=1, source_target_pairs={{2,0},{3,1},{4,2},{5,3},{6,4},{7,5},{8,6},{9,7},{10,8},{11,9},{12,... | collective-permute-start | bytes 393224 | tf_op jit(solution)/shard_map/ppermute | solution.py:12
  96.4 10.3 %copy-start.10 = (pred[16,128]{1,0:T(8,128)(4,1)S(1)}, pred[16,128]{1,0:T(8,128)(4,1)}, u32[]{:S(2)}) copy-start(pred[16,128]{1,0:T(8,128)(4,1)} %broadcast_in_dim.274) | copy-start | bytes 6148
  106.1 3.3 copy-start.8
  110.5 1.3 copy-start.7
  120.7 106.3 %copy-start.1 = (s32[64]{0:T(128)S(1)}, s32[64]{0:T(128)}, u32[]{:S(2)}) copy-start(s32[64]{0:T(128)} %param.17) | copy-start | bytes 772
  120.7 106.3 %copy-start.2 = (s32[64]{0:T(128)S(1)}, s32[64]{0:T(128)}, u32[]{:S(2)}) copy-start(s32[64]{0:T(128)} %param.16) | copy-start | bytes 772
  239.8 1.3 copy-start.3
  241.7 1.0 copy-start.4
  255.5 1.3 copy-start.3
  257.3 1.0 copy-start.4
  271.1 1.3 copy-start.3
  273.0 1.0 copy-start.4
  286.8 1.3 copy-start.3
  288.6 1.0 copy-start.4
  302.4 1.3 copy-start.3
  304.3 1.0 copy-start.4
  318.1 1.3 copy-start.3
  319.9 1.0 copy-start.4
  333.7 1.3 copy-start.3
  335.5 1.0 copy-start.4
  349.4 1.3 copy-start.3
  351.2 1.0 copy-start.4
  365.0 1.3 copy-start.3
  366.8 1.0 copy-start.4
  380.6 1.3 copy-start.3
  382.5 1.0 copy-start.4
  396.3 1.3 copy-start.3
  398.1 1.0 copy-start.4
  411.9 1.3 copy-start.3
  413.8 1.0 copy-start.4
  427.6 1.3 copy-start.3
  429.4 1.0 copy-start.4
  443.2 1.3 copy-start.3
  445.1 1.0 copy-start.4
  458.9 1.3 copy-start.3
  460.7 1.0 copy-start.4
  474.5 1.3 copy-start.3
  476.4 1.0 copy-start.4
Sparse Core Ops, SparseCore 0:
  86.9 140.0 all-gather.2
where the time goes:
time: 513 us; the launch traced here: 511 us
  local copies, waits for them, and re-layouts  137 us (27%)
  waiting for transfers between devices  114 us (22%)
  other arithmetic  89 us (17%)
  matrix products  68.6 us (13%)
  starting transfers between devices  36.4 us (7%)
  between operations  31 us (6%)
  blocking collectives  23.4 us (5%)
  loops' own time  12.5 us (2%)
    all_gather x1, waiting for transfers between devices, local(): gathered = lax.all_gather(anchor_pair, 'frame', axis=0, tiled=True)  103 us
    reduce_sum x23, other arithmetic, group_terms(): group_totals = jnp.sum(weights, axis=4)  45.4 us
    convert_element_type x16, local copies, waits for them, and re-layouts, group_terms(): weights.astype(jnp.bfloat16)  42.6 us
    while x16, matrix products  36.3 us
    all_to_all x1, blocking collectives, local(): lax.all_to_all(output, 'head', split_axis=0, concat_axis=1, tiled=True)  23.4 us
    reduce_sum x16, other arithmetic, absorb(): jnp.sum(factors[..., None] * group_sums, axis=3)  21 us
    dot_general x18, matrix products, group_terms(): jnp.einsum('qahd,gnhd->hqagn', query_blocks, key_rows, preferred_element_...  19 us
    ppermute x6, starting transfers between devices, passed_along(): return lax.ppermute(block, axis, route)  16.9 us
  transfers between devices with their start and end apart: 10, of which 3 were waited for; matrix products, arithmetic and copies ran while one was open for 10% of the time, Pallas kernels for 0%

commit v1 on v0

--- a/solution.py
+++ b/solution.py
@@ -114,7 +114,9 @@
             )
     anchor_block = (frame_blocks - offsets[frame_index] % frame_blocks) % frame_blocks
     anchor_pair = jnp.stack([key_blocks[anchor_block], value_blocks[anchor_block]])[None]
-    gathered = lax.all_gather(anchor_pair, "frame", axis=0, tiled=True)
+    gathered = jnp.concatenate(
+        lax.all_to_all(jnp.stack([anchor_pair] * lax.axis_size("frame")), "frame", 0, 0), axis=0
+    )
     piece_frames = gathered.shape[0]
     group_width = 4
     grouped = gathered.reshape(

time: 513 us -> 553 us (1.078)
  waiting for transfers between devices: 114 us -> 154 us
  starting transfers between devices: 36.4 us -> 59.1 us
  between operations: 31 us -> 17.6 us
  blocking collectives: 23.4 us -> 16.6 us
    ppermute x6, waiting for transfers between devices: 7.73 us -> 131 us  [passed_along(): return lax.ppermute(block, axis, route)]
    all_gather x1 -> x0, waiting for transfers between devices: 103 us -> none  [local(): gathered = lax.all_gather(anchor_pair, 'frame', axis=0, tiled=True)]
    all_to_all x0 -> x1, starting transfers between devices: none -> 14.4 us  [local(): lax.all_to_all(jnp.stack([anchor_pair] * lax.axis_size('frame')), 'frame'...]
    ppermute x6, starting transfers between devices: 16.9 us -> 25.8 us  [passed_along(): return lax.ppermute(block, axis, route)]
    all_to_all x1, waiting for transfers between devices: 0.01 us -> 7.41 us  [local(): lax.all_to_all(keys, 'head', split_axis=1, concat_axis=0, tiled=True)]
    all_to_all x1, blocking collectives: 23.4 us -> 16.6 us  [local(): lax.all_to_all(output, 'head', split_axis=0, concat_axis=1, tiled=True)]
    all_to_all x1, waiting for transfers between devices: 0.01 us -> 6.65 us  [local(): lax.all_to_all(queries, 'head', split_axis=1, concat_axis=0, tiled=True)]
    all_to_all x1, waiting for transfers between devices: 2.51 us -> 8.45 us  [local(): lax.all_to_all(values, 'head', split_axis=1, concat_axis=0, tiled=True)]
  transfers between devices with their start and end apart: 10 -> 10, of which waited for: 3 -> 4; matrix products, arithmetic and copies ran while one was open for 10% -> 8% of each run, Pallas kernels for 0% -> 0%
where the time goes in v1:
time: 553 us; the launch traced here: 549 us
  waiting for transfers between devices  154 us (28%)
  local copies, waits for them, and re-layouts  134 us (24%)
  other arithmetic  88.3 us (16%)
  matrix products  67.5 us (12%)
  starting transfers between devices  59.1 us (11%)
  between operations  17.6 us (3%)
  blocking collectives  16.6 us (3%)
  loops' own time  12.5 us (2%)
    ppermute x6, waiting for transfers between devices, passed_along(): return lax.ppermute(block, axis, route)  131 us
    reduce_sum x23, other arithmetic, group_terms(): group_totals = jnp.sum(weights, axis=4)  45 us
    convert_element_type x16, local copies, waits for them, and re-layouts, group_terms(): weights.astype(jnp.bfloat16)  42.6 us
    while x16, matrix products  36.3 us
    ppermute x6, starting transfers between devices, passed_along(): return lax.ppermute(block, axis, route)  25.8 us
    reduce_sum x16, other arithmetic, absorb(): jnp.sum(factors[..., None] * group_sums, axis=3)  21.3 us
    dot_general x18, matrix products, group_terms(): jnp.einsum('qahd,gnhd->hqagn', query_blocks, key_rows, preferred_element_...  17.9 us
    while x80, local copies, waits for them, and re-layouts  17.1 us
  transfers between devices with their start and end apart: 10, of which 4 were waited for; matrix products, arithmetic and copies ran while one was open for 8% of the time, Pallas kernels for 0%

profile of v1, /device:TPU:1, one launch (start us, length us, event | category | flops | bytes accessed | tf_op | source)
XLA Modules:
  0.0 549.1 jit_solution(17221768444950155614)
XLA Ops:
  2.0 10.2 %all-to-all-start.1 = ((bf16[128,16,128]{2,0,1:T(8,128)(2,1)}), bf16[128,16,128]{2,0,1:T(8,128)(2,1)S(1)}, u32[]{:S(2)}, u32[]{:S(2)}) async-start(bf16[128,16,128]{2,0,1:T(8,128)(2,1)} %copy.120), calls=%async_computation.1 | async-start | bytes 1048576 | tf_op jit(solution)/shard_map/all_to_all | solution.py:53
  14.2 7.4 %all-to-all-done.1 = bf16[128,16,128]{2,0,1:T(8,128)(2,1)S(1)} async-done(((bf16[128,16,128]{2,0,1:T(8,128)(2,1)}), bf16[128,16,128]{2,0,1:T(8,128)(2,1)S(1)}, u32[]{:S(2)}, u32[]{:S(2)}) %all-to-all-start.1) | async-done | bytes 524320 | tf_op jit(solution)/shard_map/all_to_all | solution.py:53
  21.7 4.4 all-to-all-start.2
  27.0 8.4 %all-to-all-done.2 = bf16[128,16,128]{2,0,1:T(8,128)(2,1)S(1)} async-done(((bf16[128,16,128]{2,0,1:T(8,128)(2,1)}), bf16[128,16,128]{2,0,1:T(8,128)(2,1)S(1)}, u32[]{:S(2)}, u32[]{:S(2)}) %all-to-all-start.2) | async-done | bytes 524320 | tf_op jit(solution)/shard_map/all_to_all | solution.py:54
  35.4 4.4 all-to-all-start
  42.5 6.7 %all-to-all-done = bf16[128,16,128]{2,0,1:T(8,128)(2,1)S(1)} async-done(((bf16[128,16,128]{2,0,1:T(8,128)(2,1)}), bf16[128,16,128]{2,0,1:T(8,128)(2,1)S(1)}, u32[]{:S(2)}, u32[]{:S(2)}) %all-to-all-start) | async-done | bytes 524320 | tf_op jit(solution)/shard_map/all_to_all | solution.py:52
  49.1 3.0 stack.34
  52.2 14.4 %all-to-all-start.3 = ((bf16[64,1,2,64,2,128]{5,3,4,2,1,0:T(8,128)(2,1)}), bf16[64,1,2,64,2,128]{5,3,4,2,1,0:T(8,128)(2,1)}, u32[]{:S(2)}, u32[]{:S(2)}) async-start(bf16[64,1,2,64,2,128]{5,3,4,2,1,0:T(8,128)(2,1)} %stack.34), calls=%async_computation.3 | async-start | bytes 8388608 | tf_op jit(solution)/shard_map/all_to_all | solution.py:118
  96.8 5.8 %collective-permute-start.4 = (bf16[2,2,64,2,128]{4,2,3,1,0:T(8,128)(2,1)S(1)}, bf16[2,2,64,2,128]{4,2,3,1,0:T(8,128)(2,1)S(1)}, u32[]{:S(2)}, u32[]{:S(2)}) collective-permute-start(bf16[2,2,64,2,128]{4,2,3,1,0:T(8,128)(2,1)S(1)} %pad_maximum_fusion.1), channel_id=1, source_target_pairs={{0,3},{1,4},{2,5},{3,6},{4,7},{5,8},{6,9},{7,10},{8,11},{9,12},{10... | collective-permute-start | bytes 393224 | tf_op jit(solution)/shard_map/ppermute | solution.py:12
  103.9 5.6 %collective-permute-start.2 = (bf16[2,2,64,2,128]{4,2,3,1,0:T(8,128)(2,1)S(1)}, bf16[2,2,64,2,128]{4,2,3,1,0:T(8,128)(2,1)S(1)}, u32[]{:S(2)}, u32[]{:S(2)}) collective-permute-start(bf16[2,2,64,2,128]{4,2,3,1,0:T(8,128)(2,1)S(1)} %pad_maximum_fusion.1), channel_id=1, source_target_pairs={{0,2},{1,3},{2,4},{3,5},{4,6},{5,7},{6,8},{7,9},{8,10},{9,11},{10,... | collective-permute-start | bytes 393224 | tf_op jit(solution)/shard_map/ppermute | solution.py:12
  113.4 2.6 fusion.21
  117.4 131.3 %collective-permute-done.5 = bf16[2,2,64,2,128]{4,2,3,1,0:T(8,128)(2,1)S(1)} collective-permute-done((bf16[2,2,64,2,128]{4,2,3,1,0:T(8,128)(2,1)S(1)}, bf16[2,2,64,2,128]{4,2,3,1,0:T(8,128)(2,1)S(1)}, u32[]{:S(2)}, u32[]{:S(2)}) %collective-permute-start.5) | collective-permute-done | bytes 131104 | tf_op jit(solution)/shard_map/ppermute | solution.py:12
  248.7 10.5 %collective-permute-start = (bf16[2,4,64,2,128]{4,2,3,1,0:T(8,128)(2,1)S(1)}, bf16[2,4,64,2,128]{4,2,3,1,0:T(8,128)(2,1)S(1)}, u32[]{:S(2)}, u32[]{:S(2)}) collective-permute-start(bf16[2,4,64,2,128]{4,2,3,1,0:T(8,128)(2,1)S(1)} %pad_maximum_fusion), channel_id=1, source_target_pairs={{0,1},{1,2},{2,3},{3,4},{4,5},{5,6},{6,7},{7,8},{8,9},{9,10},{10,1... | collective-permute-start | bytes 786440 | tf_op jit(solution)/shard_map/ppermute | solution.py:12
  274.9 3.0 fusion.58
  277.9 251.2 %while.16 = (s32[]{:T(128)}, f32[2,16,64]{2,1,0:T(8,128)S(1)}, f32[2,16,64]{2,1,0:T(8,128)S(1)}, f32[2,16,64,128]{3,2,1,0:T(8,128)}, s32[]{:T(128)}, /*index=5*/...) while((s32[]{:T(128)}, f32[2,16,64]{2,1,0:T(8,128)S(1)}, ...), condition=%wide.region_22.25_spmd, body=%wide.region_16.24_spmd.sunk | while | flops 276053440 | bytes 31036728 | solution.py:142
  283.3 2.4 fusion.229
  285.8 2.7 copy.174
  288.4 2.3 fusion.230
  299.0 2.4 fusion.229
  301.5 2.7 copy.174
  304.1 2.3 fusion.230
  314.7 2.4 fusion.229
  317.1 2.7 copy.174
  319.8 2.3 fusion.230
  330.4 2.4 fusion.229
  332.8 2.7 copy.174
  335.5 2.3 fusion.230
  346.1 2.4 fusion.229
  348.5 2.7 copy.174
  351.2 2.3 fusion.230
  361.8 2.4 fusion.229
  364.2 2.7 copy.174
  366.9 2.3 fusion.230
  377.5 2.4 fusion.229
  379.9 2.7 copy.174
  382.6 2.3 fusion.230
  393.2 2.4 fusion.229
  395.6 2.7 copy.174
  398.3 2.3 fusion.230
  408.9 2.4 fusion.229
  411.3 2.7 copy.174
  414.0 2.3 fusion.230
  424.6 2.4 fusion.229
  427.0 2.7 copy.174
  429.7 2.3 fusion.230
  440.3 2.4 fusion.229
  442.7 2.7 copy.174
  445.4 2.3 fusion.230
  456.0 2.4 fusion.229
  458.4 2.7 copy.174
  461.1 2.3 fusion.230
  471.7 2.4 fusion.229
  474.1 2.7 copy.174
  476.8 2.3 fusion.230
  487.4 2.4 fusion.229
  489.8 2.7 copy.174
  492.5 2.3 fusion.230
  503.1 2.4 fusion.229
  505.5 2.7 copy.174
  508.2 2.3 fusion.230
  518.8 2.4 fusion.229
  521.2 2.7 copy.174
  523.9 2.3 fusion.230
  531.2 16.6 %all_to_all.68 = bf16[1024,2,128]{2,1,0:T(2,128)(2,1)S(1)} all-to-all(bf16[1024,2,128]{2,1,0:T(2,128)(2,1)S(1)} %bitcast.475), channel_id=1, replica_groups=mesh['head'=8,'frame'=64] {'head'}, dimensions={0} | all-to-all | bytes 1048576 | tf_op jit(solution)/shard_map/all_to_all | solution.py:147
  (537 shorter events, 168.2 us)
Async XLA Ops:
  0.0 82.1 %copy-start = (s32[64,16,16]{0,2,1:T(8,128)S(1)}, s32[64,16,16]{0,2,1:T(8,128)}, u32[]{:S(2)}) copy-start(s32[64,16,16]{0,2,1:T(8,128)} %param.15) | copy-start | bytes 196612
  0.0 26.0 %copy-start.5 = (bf16[128,16,128]{2,1,0:T(8,128)(2,1)S(1)}, bf16[128,16,128]{2,1,0:T(8,128)(2,1)}, u32[]{:S(2)}) copy-start(bf16[128,16,128]{2,1,0:T(8,128)(2,1)} %param.12) | copy-start | bytes 1572868
  0.0 39.8 %copy-start.1 = (s32[64]{0:T(128)S(1)}, s32[64]{0:T(128)}, u32[]{:S(2)}) copy-start(s32[64]{0:T(128)} %param.17) | copy-start | bytes 772
  2.0 19.6 %all-to-all-start.1 = ((bf16[128,16,128]{2,0,1:T(8,128)(2,1)}), bf16[128,16,128]{2,0,1:T(8,128)(2,1)S(1)}, u32[]{:S(2)}, u32[]{:S(2)}) async-start(bf16[128,16,128]{2,0,1:T(8,128)(2,1)} %copy.120), calls=%async_computation.1 | async-start | bytes 1048576 | tf_op jit(solution)/shard_map/all_to_all | solution.py:53
  21.7 13.7 %all-to-all-start.2 = ((bf16[128,16,128]{2,0,1:T(8,128)(2,1)}), bf16[128,16,128]{2,0,1:T(8,128)(2,1)S(1)}, u32[]{:S(2)}, u32[]{:S(2)}) async-start(bf16[128,16,128]{2,0,1:T(8,128)(2,1)} %copy.126), calls=%async_computation.2 | async-start | bytes 1048576 | tf_op jit(solution)/shard_map/all_to_all | solution.py:54
  35.4 13.7 %all-to-all-start = ((bf16[128,16,128]{2,0,1:T(8,128)(2,1)}), bf16[128,16,128]{2,0,1:T(8,128)(2,1)S(1)}, u32[]{:S(2)}, u32[]{:S(2)}) async-start(bf16[128,16,128]{2,0,1:T(8,128)(2,1)} %copy.118), calls=%async_computation | async-start | bytes 1048576 | tf_op jit(solution)/shard_map/all_to_all | solution.py:52
  52.2 25.5 %copy-start.2 = (s32[64]{0:T(128)S(1)}, s32[64]{0:T(128)}, u32[]{:S(2)}) copy-start(s32[64]{0:T(128)} %param.16) | copy-start | bytes 772
  52.2 225.7 %all-to-all-start.3 = ((bf16[64,1,2,64,2,128]{5,3,4,2,1,0:T(8,128)(2,1)}), bf16[64,1,2,64,2,128]{5,3,4,2,1,0:T(8,128)(2,1)}, u32[]{:S(2)}, u32[]{:S(2)}) async-start(bf16[64,1,2,64,2,128]{5,3,4,2,1,0:T(8,128)(2,1)} %stack.34), calls=%async_computation.3 | async-start | bytes 8388608 | tf_op jit(solution)/shard_map/all_to_all | solution.py:118
  95.5 153.2 %collective-permute-start.5 = (bf16[2,2,64,2,128]{4,2,3,1,0:T(8,128)(2,1)S(1)}, bf16[2,2,64,2,128]{4,2,3,1,0:T(8,128)(2,1)S(1)}, u32[]{:S(2)}, u32[]{:S(2)}) collective-permute-start(bf16[2,2,64,2,128]{4,2,3,1,0:T(8,128)(2,1)S(1)} %pad_maximum_fusion.1), channel_id=1, source_target_pairs={{3,0},{4,1},{5,2},{6,3},{7,4},{8,5},{9,6},{10,7},{11,8},{12,9},{13... | collective-permute-start | bytes 393224 | tf_op jit(solution)/shard_map/ppermute | solution.py:12
  96.8 162.5 %collective-permute-start.4 = (bf16[2,2,64,2,128]{4,2,3,1,0:T(8,128)(2,1)S(1)}, bf16[2,2,64,2,128]{4,2,3,1,0:T(8,128)(2,1)S(1)}, u32[]{:S(2)}, u32[]{:S(2)}) collective-permute-start(bf16[2,2,64,2,128]{4,2,3,1,0:T(8,128)(2,1)S(1)} %pad_maximum_fusion.1), channel_id=1, source_target_pairs={{0,3},{1,4},{2,5},{3,6},{4,7},{5,8},{6,9},{7,10},{8,11},{9,12},{10... | collective-permute-start | bytes 393224 | tf_op jit(solution)/shard_map/ppermute | solution.py:12
  102.6 156.7 %collective-permute-start.3 = (bf16[2,2,64,2,128]{4,2,3,1,0:T(8,128)(2,1)S(1)}, bf16[2,2,64,2,128]{4,2,3,1,0:T(8,128)(2,1)S(1)}, u32[]{:S(2)}, u32[]{:S(2)}) collective-permute-start(bf16[2,2,64,2,128]{4,2,3,1,0:T(8,128)(2,1)S(1)} %pad_maximum_fusion.1), channel_id=1, source_target_pairs={{2,0},{3,1},{4,2},{5,3},{6,4},{7,5},{8,6},{9,7},{10,8},{11,9},{12,... | collective-permute-start | bytes 393224 | tf_op jit(solution)/shard_map/ppermute | solution.py:12
  103.9 155.4 %collective-permute-start.2 = (bf16[2,2,64,2,128]{4,2,3,1,0:T(8,128)(2,1)S(1)}, bf16[2,2,64,2,128]{4,2,3,1,0:T(8,128)(2,1)S(1)}, u32[]{:S(2)}, u32[]{:S(2)}) collective-permute-start(bf16[2,2,64,2,128]{4,2,3,1,0:T(8,128)(2,1)S(1)} %pad_maximum_fusion.1), channel_id=1, source_target_pairs={{0,2},{1,3},{2,4},{3,5},{4,6},{5,7},{6,8},{7,9},{8,10},{9,11},{10,... | collective-permute-start | bytes 393224 | tf_op jit(solution)/shard_map/ppermute | solution.py:12
  116.1 148.5 %collective-permute-start.1 = (bf16[2,4,64,2,128]{4,2,3,1,0:T(8,128)(2,1)S(1)}, bf16[2,4,64,2,128]{4,2,3,1,0:T(8,128)(2,1)S(1)}, u32[]{:S(2)}, u32[]{:S(2)}) collective-permute-start(bf16[2,4,64,2,128]{4,2,3,1,0:T(8,128)(2,1)S(1)} %pad_maximum_fusion), channel_id=1, source_target_pairs={{1,0},{2,1},{3,2},{4,3},{5,4},{6,5},{7,6},{8,7},{9,8},{10,9},{11,1... | collective-permute-start | bytes 786440 | tf_op jit(solution)/shard_map/ppermute | solution.py:12
  248.7 16.1 %collective-permute-start = (bf16[2,4,64,2,128]{4,2,3,1,0:T(8,128)(2,1)S(1)}, bf16[2,4,64,2,128]{4,2,3,1,0:T(8,128)(2,1)S(1)}, u32[]{:S(2)}, u32[]{:S(2)}) collective-permute-start(bf16[2,4,64,2,128]{4,2,3,1,0:T(8,128)(2,1)S(1)} %pad_maximum_fusion), channel_id=1, source_target_pairs={{0,1},{1,2},{2,3},{3,4},{4,5},{5,6},{6,7},{7,8},{8,9},{9,10},{10,1... | collective-permute-start | bytes 786440 | tf_op jit(solution)/shard_map/ppermute | solution.py:12
  290.7 1.3 copy-start.3
  292.5 1.1 copy-start.4
  306.4 1.3 copy-start.3
  308.2 1.1 copy-start.4
  322.1 1.3 copy-start.3
  323.9 1.1 copy-start.4
  337.8 1.3 copy-start.3
  339.6 1.1 copy-start.4
  353.5 1.3 copy-start.3
  355.3 1.1 copy-start.4
  369.2 1.3 copy-start.3
  371.0 1.1 copy-start.4
  384.9 1.3 copy-start.3
  386.7 1.1 copy-start.4
  400.6 1.3 copy-start.3
  402.4 1.1 copy-start.4
  416.3 1.3 copy-start.3
  418.1 1.1 copy-start.4
  432.0 1.3 copy-start.3
  433.8 1.1 copy-start.4
  447.7 1.3 copy-start.3
  449.5 1.1 copy-start.4
  463.4 1.3 copy-start.3
  465.2 1.1 copy-start.4
  479.1 1.3 copy-start.3
  480.9 1.1 copy-start.4
  494.8 1.3 copy-start.3
  496.6 1.1 copy-start.4
  510.4 1.3 copy-start.3
  512.3 1.1 copy-start.4
  526.1 1.3 copy-start.3
  528.0 1.1 copy-start.4
